TPU v7x, 32 devices: a whole 2x2x4 slice. The times are simulated.
32 devices in a mesh: dp: 2 (over core), shard: 16 (over z, y, x).
Axes of the slice: x: 2, y: 2, z: 4, core: 2. Of those that a mesh axis runs over, the one named last changes fastest.
Arguments:
- hidden_in: bfloat16 [4096, 1024], P(('dp', 'shard')), may hold values from -6 to 6
- doc_ids: int32 [32, 128], P(('dp', 'shard')), may hold values from 0 to 3, never falling along the last dimension, each value on 1 to 64 neighbouring positions
- expert_ids: int32 [4096], P(('dp', 'shard')), may hold values from 0 to 1, as said below
- slot_ids: int32 [4096], P(('dp', 'shard')), may hold values from 0 to 73, as said below
- out_grad: bfloat16 [4096, 1024], P(('dp', 'shard')), may hold values from -6 to 6
- ln1_gain: bfloat16 [1024], P(('dp', 'shard')), may hold values from 0.5 to 1.5
- ln1_bias: bfloat16 [1024], P(('dp', 'shard')), may hold values from -1 to 1
- w_query: bfloat16 [1024, 1024], P(('dp', 'shard')), may hold values from -0.1875 to 0.1875
- w_key: bfloat16 [1024, 1024], P(('dp', 'shard')), may hold values from -0.1875 to 0.1875
- w_value: bfloat16 [1024, 1024], P(('dp', 'shard')), may hold values from -0.1875 to 0.1875
- w_out: bfloat16 [1024, 1024], P(('dp', 'shard')), may hold values from -0.5 to 0.5
- ln2_gain: bfloat16 [1024], P(('dp', 'shard')), may hold values from 0.5 to 1.5
- ln2_bias: bfloat16 [1024], P(('dp', 'shard')), may hold values from -1 to 1
- w_up: bfloat16 [1024, 4096], P(('dp', 'shard')), may hold values from -0.1875 to 0.1875
- w_down: bfloat16 [4096, 1024], P(('dp', 'shard')), may hold values from -0.09375 to 0.09375
- w_router: bfloat16 [1024, 2], P(('dp', 'shard')), may hold values from -0.125 to 0.125
- w_mix: bfloat16 [1024, 2], P(('dp', 'shard')), may hold values from -0.1875 to 0.1875
- expert_up: bfloat16 [2, 1024, 4096], P(None, ('dp', 'shard')), may hold values from -0.1875 to 0.1875
- expert_down: bfloat16 [2, 4096, 1024], P(None, ('dp', 'shard')), may hold values from -0.09375 to 0.09375
- load_avg: float32 [2], replicated, may hold values from 0.05 to 0.3
Outputs:
- layer_out: bfloat16 [4096, 1024], P(('dp', 'shard'))
- input_grad: bfloat16 [4096, 1024], P(('dp', 'shard'))
- grad_ln1_gain: float32 [1024], P(('dp', 'shard'))
- grad_ln1_bias: float32 [1024], P(('dp', 'shard'))
- grad_w_query: float32 [1024, 1024], P(('dp', 'shard'))
- grad_w_key: float32 [1024, 1024], P(('dp', 'shard'))
- grad_w_value: float32 [1024, 1024], P(('dp', 'shard'))
- grad_w_out: float32 [1024, 1024], P(('dp', 'shard'))
- grad_ln2_gain: float32 [1024], P(('dp', 'shard'))
- grad_ln2_bias: float32 [1024], P(('dp', 'shard'))
- grad_w_up: float32 [1024, 4096], P(('dp', 'shard'))
- grad_w_down: float32 [4096, 1024], P(('dp', 'shard'))
- grad_w_router: float32 [1024, 2], P(('dp', 'shard'))
- grad_w_mix: float32 [1024, 2], P(('dp', 'shard'))
- grad_expert_up: float32 [2, 1024, 4096], P(None, ('dp', 'shard'))
- grad_expert_down: float32 [2, 4096, 1024], P(None, ('dp', 'shard'))
- expert_counts: int32 [2], replicated
- load_avg_new: float32 [2], replicated
Inputs may be any that keep to these rules, and one draw needn't show every extreme that they name: `expert_ids`: of the 128 tokens of one sequence at most 74 go to one expert, and in some sequence exactly 74 do. `slot_ids`: A token's slot is the number of earlier tokens of the same sequence routed to the same expert.
All inputs are finite; a program needn't handle non-finite values.
Results may differ from a plain program's by a relative error of at most 0.012.
The roundings to bfloat16 on the way count: a program that leaves them out, or rounds other values in their place, can miss the bound.
Values may be sent and summed in bfloat16 or wider, within the bound.
A program may use at most 384 MiB of HBM per device.

v0:
```python
import jax
import jax.numpy as jnp
from jax import lax
from jax.sharding import PartitionSpec as P

HEADS = 16
CAP = 74
BF = jnp.bfloat16
F32 = jnp.float32
BOTH = ("dp", "shard")


def mm(a, b, dims=((1,), (0,))):
    return lax.dot_general(a, b, (dims, ((), ())), preferred_element_type=F32)


def layer_norm(values, gain, bias):
    centre = values - jnp.mean(values, axis=-1, keepdims=True)
    scale_inv = lax.rsqrt(jnp.mean(centre * centre, axis=-1, keepdims=True) + 1e-05)
    normed = centre * scale_inv
    return (normed * gain + bias, normed, scale_inv)


def norm_back(grad_out, normed, scale_inv, gain):
    grad_normed = grad_out * gain
    inner = grad_normed - jnp.mean(grad_normed, axis=-1, keepdims=True)
    inner = inner - normed * jnp.mean(grad_normed * normed, axis=-1, keepdims=True)
    return (scale_inv * inner, jnp.sum(grad_out * normed, axis=0), jnp.sum(grad_out, axis=0))


def gelu_pair(t):
    inner = 0.7978845608 * (t + 0.044715 * t * t * t)
    th = jnp.tanh(inner)
    val = 0.5 * t * (1.0 + th)
    der = 0.5 * (1.0 + th) + 0.5 * t * (1.0 - th * th) * 0.7978845608 * (
        1.0 + 3.0 * 0.044715 * t * t
    )
    return (val, der)


def ag(block):
    return lax.all_gather(block, "shard", axis=0, tiled=False)


def rs(parts):
    return lax.psum_scatter(parts.astype(BF), "shard", scatter_dimension=0, tiled=False).astype(F32)


def body(
    hidden_in,
    doc_ids,
    expert_ids,
    slot_ids,
    out_grad,
    ln1_gain,
    ln1_bias,
    w_query,
    w_key,
    w_value,
    w_out,
    ln2_gain,
    ln2_bias,
    w_up,
    w_down,
    w_router,
    w_mix,
    expert_up,
    expert_down,
    load_avg,
):
    T, D = hidden_in.shape
    H, HD = (HEADS, D // HEADS)
    S = lax.axis_size("shard")
    C = lax.axis_size("dp")
    WR = w_query.shape[0]
    FF = w_up.shape[1]
    FR = w_down.shape[0]
    F = FR * C
    E = expert_up.shape[0]
    LO, HI = (80, T - 80)
    pos = jnp.where(
        expert_ids == 0, slot_ids, jnp.sum((expert_ids == 0).astype(jnp.int32)) + slot_ids
    )
    n0 = jnp.sum((expert_ids == 0).astype(jnp.int32))
    place = lax.iota(jnp.int32, T)
    perm = (pos[None, :] == place[:, None]).astype(BF)
    xs = mm(perm, hidden_in)
    dys = mm(perm, out_grad).astype(BF)
    doc = doc_ids[0]
    allowed = (place[None, :] <= place[:, None]) & (doc[:, None] == doc[None, :])
    allowed = mm(mm(perm, allowed.astype(BF)).astype(BF), perm, ((1,), (1,))) > 0.5
    is0 = (place < n0)[:, None]
    small = jnp.stack(
        [
            ln1_gain,
            ln1_bias,
            ln2_gain,
            ln2_bias,
            w_router[:, 0],
            w_router[:, 1],
            w_mix[:, 0],
            w_mix[:, 1],
        ]
    ).astype(F32)
    small = lax.all_gather(small, BOTH, axis=1, tiled=True)
    g1, b1, g2, b2 = (small[0], small[1], small[2], small[3])
    wr, wm = (small[4:6], small[6:8])
    wa = jnp.stack([w_query, w_key, w_value, w_out])
    wa = lax.all_gather(wa, BOTH, axis=1, tiled=True)
    wq, wk, wv, wo = (wa[0], wa[1], wa[2], wa[3])
    ups = jnp.stack([w_up, expert_up[0], expert_up[1]])
    ups = ups.reshape(3, WR, C, S, FR).transpose(3, 0, 1, 2, 4).reshape(S, 3, WR, F)
    ups = lax.all_to_all(ups, "shard", 0, 0)
    ups = lax.all_gather(ups, "dp", axis=0)
    ups = ups.transpose(2, 0, 1, 3, 4).reshape(3, D, F)
    downs = jnp.stack([w_down, expert_down[0], expert_down[1]])
    downs = lax.all_gather(downs, "dp", axis=1, tiled=True)
    dy_all = ag(dys)
    n1, u1, i1 = layer_norm(xs, g1, b1)
    h1b = n1.astype(BF)
    q = (mm(h1b, wq) * 0.125).astype(BF).reshape(T, H, HD)
    k = mm(h1b, wk).astype(BF).reshape(T, H, HD)
    v = mm(h1b, wv).astype(BF).reshape(T, H, HD)
    s = jnp.einsum("ihd,jhd->hij", q, k, preferred_element_type=F32)
    s = jnp.where(allowed[None], s, -1e30)
    ex = jnp.exp(s - jnp.max(s, axis=-1, keepdims=True))
    p = ex / jnp.sum(ex, axis=-1, keepdims=True)
    pb = p.astype(BF)
    o = jnp.einsum("hij,jhd->ihd", pb, v, preferred_element_type=F32).reshape(T, D).astype(BF)
    x1 = xs + mm(o, wo)
    h2, u2, i2 = layer_norm(x1, g2, b2)
    h2b = h2.astype(BF)

    def two(w):
        return jnp.stack([jnp.sum(h2 * w[0], axis=-1), jnp.sum(h2 * w[1], axis=-1)], axis=-1)

    r = jax.nn.softmax(two(wr), axis=-1)
    c = jax.nn.softmax(two(wm), axis=-1)
    gate = jnp.where(is0, r[:, 0:1], r[:, 1:2])
    c0, c1 = (c[:, 0:1], c[:, 1:2])
    we = c0 * gate
    scal = jnp.concatenate([c1, jnp.where(is0, we, 0.0), jnp.where(is0, 0.0, we)], axis=1)
    h_all = ag(h2b)
    scal_all = ag(scal)

    def cut(a, e):
        return (a[:, :LO] if e == 1 else a[:, HI:]) if e else a

    partial_y = jnp.zeros((S, T, D), F32)
    partial_dh = jnp.zeros((S, T, D), F32)
    score = []
    gup, gdown = ([], [])
    for e in range(3):
        he = cut(h_all, e)
        dye = cut(dy_all, e).astype(F32)
        se = cut(scal_all, e)[:, :, e : e + 1]
        n = he.shape[1]
        hf = he.reshape(S * n, D)
        pre = mm(hf, ups[e])
        val, der = gelu_pair(pre)
        ub = val.astype(BF)
        m = mm(ub, downs[e]).reshape(S, n, D)
        dm = (dye * se).astype(BF).reshape(S * n, D)
        dg = (mm(dm, downs[e], ((1,), (1,))) * der).astype(BF)
        gdown.append(mm(ub, dm, ((0,), (0,))))
        gup.append(mm(hf, dg, ((0,), (0,))))
        dx = mm(dg, ups[e], ((1,), (1,))).reshape(S, n, D)
        y = m * se
        sc = jnp.sum(dye * m, axis=-1)
        pad = [(0, 0), (0, T - n) if e < 2 else (T - n, 0)]
        live = is0[None, :, 0]
        partial_y += jnp.pad(y, pad + [(0, 0)])
        partial_dh += jnp.pad(dx, pad + [(0, 0)])
        score.append(jnp.pad(sc, pad))
    yfull = rs(partial_y)
    dh2 = rs(partial_dh)
    sc = lax.psum_scatter(jnp.stack(score, axis=1), "shard", scatter_dimension=0, tiled=False)
    sm = sc[0][:, None]
    se = jnp.where(is0, sc[1][:, None], sc[2][:, None])
    dc0, dc1 = (gate * se, sm)
    tot = c0 * dc0 + c1 * dc1
    dcl0, dcl1 = (c0 * (dc0 - tot), c1 * (dc1 - tot))
    dgate = c0 * se
    dr0, dr1 = (jnp.where(is0, dgate, 0.0), jnp.where(is0, 0.0, dgate))
    tot = r[:, 0:1] * dr0 + r[:, 1:2] * dr1
    drl0, drl1 = (r[:, 0:1] * (dr0 - tot), r[:, 1:2] * (dr1 - tot))
    layer_out = (x1 + yfull).astype(BF)
    dh2 = dh2 + drl0 * wr[0] + drl1 * wr[1] + dcl0 * wm[0] + dcl1 * wm[1]
    gw = [jnp.sum(h2 * t, axis=0) for t in (drl0, drl1, dcl0, dcl1)]
    dx1, gg2, gb2 = norm_back(dh2, u2, i2, g2)
    dx1 = dx1 + dys.astype(F32)
    dab = dx1.astype(BF)
    gwo = mm(o, dab, ((0,), (0,)))
    do = mm(dab, wo, ((1,), (1,))).astype(BF).reshape(T, H, HD)
    dp = jnp.einsum("ihd,jhd->hij", do, v, preferred_element_type=F32)
    ds = (p * (dp - jnp.sum(p * dp, axis=-1, keepdims=True))).astype(BF)
    dq = jnp.einsum("hij,jhd->ihd", ds, k, preferred_element_type=F32).astype(BF)
    dq = (dq * BF(0.125)).reshape(T, D)
    dk = jnp.einsum("hij,ihd->jhd", ds, q, preferred_element_type=F32).astype(BF).reshape(T, D)
    dv = jnp.einsum("hij,ihd->jhd", pb, do, preferred_element_type=F32).astype(BF).reshape(T, D)
    dh1 = mm(dq, wq, ((1,), (1,))) + mm(dk, wk, ((1,), (1,))) + mm(dv, wv, ((1,), (1,)))
    ga = jnp.stack(
        [mm(h1b, dq, ((0,), (0,))), mm(h1b, dk, ((0,), (0,))), mm(h1b, dv, ((0,), (0,))), gwo]
    )
    dxn, gg1, gb1 = norm_back(dh1, u1, i1, g1)
    input_grad = (dx1 + dxn).astype(BF)
    layer_out = mm(perm, layer_out, ((0,), (0,))).astype(BF)
    input_grad = mm(perm, input_grad, ((0,), (0,))).astype(BF)
    smalls = lax.psum(jnp.stack([gg1, gb1, gg2, gb2] + gw), BOTH)
    mine = lax.dynamic_slice_in_dim(smalls, lax.axis_index(BOTH) * WR, WR, 1)
    ga = ga.reshape(4, C, S, WR, D).transpose(1, 2, 0, 3, 4)
    ga = lax.psum_scatter(ga.astype(BF), "dp", scatter_dimension=0, tiled=False)
    ga = lax.psum_scatter(ga, "shard", scatter_dimension=0, tiled=False).astype(F32)
    gdown = lax.psum_scatter(jnp.stack(gdown), "dp", scatter_dimension=1, tiled=True)
    gup = jnp.stack(gup).reshape(3, C, S, WR, F).transpose(1, 2, 0, 3, 4)
    gup = lax.psum_scatter(gup, "dp", scatter_dimension=0, tiled=False).astype(BF)
    gup = lax.all_to_all(gup, "shard", 0, 0).astype(F32)
    gup = gup.reshape(S, 3, WR, C, FR).transpose(1, 2, 3, 0, 4).reshape(3, WR, FF)
    counts = lax.psum(jnp.stack([n0, T - n0]), BOTH)
    load_new = 0.9 * load_avg + 0.1 * counts.astype(F32) * E / (T * C * S)
    return (
        layer_out,
        input_grad,
        mine[0],
        mine[1],
        ga[0],
        ga[1],
        ga[2],
        ga[3],
        mine[2],
        mine[3],
        gup[0],
        gdown[0],
        jnp.stack([mine[4], mine[5]], axis=1),
        jnp.stack([mine[6], mine[7]], axis=1),
        gup[1:],
        gdown[1:],
        counts,
        load_new,
    )


def solution(mesh):
    row, vec = (P(BOTH, None), P(BOTH))
    mid = P(None, BOTH, None)
    return jax.shard_map(
        body,
        mesh=mesh,
        in_specs=(
            row,
            row,
            vec,
            vec,
            row,
            vec,
            vec,
            row,
            row,
            row,
            row,
            vec,
            vec,
            row,
            row,
            row,
            row,
            mid,
            mid,
            P(),
        ),
        out_specs=(
            row,
            row,
            vec,
            vec,
            row,
            row,
            row,
            row,
            vec,
            vec,
            row,
            row,
            row,
            row,
            mid,
            mid,
            P(),
            P(),
        ),
        check_vma=False,
    )
```

profile of v0, /device:TPU:0, one launch (start us, length us, event | category | flops | bytes accessed | tf_op | source)
XLA Modules:
  0.0 906.7 jit_solution(14686394213423674145)
XLA Ops:
  7.3 1.7 pad_maximum_fusion.2
  9.0 1.1 copy.128
  12.2 1.4 reshape.288
  13.6 8.3 all-to-all-start
  22.1 81.6 %all-gather.4 = f32[32,32,8]{1,2,0:T(8,128)S(1)} all-gather(f32[1,32,8]{1,2,0:T(8,128)S(1)} %convert_bitcast_fusion.4), channel_id=1, replica_groups=mesh['dp'=2,'shard'=16] {'dp','shard'}, dimensions={0}, use_global_device_ids=true | all-gather | bytes 33792 | tf_op jit(solution)/shard_map/all_gather | solution.py:105
  107.2 2.1 fusion.40
  109.5 2.2 fusion.42
  111.8 2.4 fusion.41
  114.4 1.5 fusion.117
  116.6 2.1 fusion.118
  123.3 1.6 copy.132
  125.9 70.1 %all-gather.15.cloned.1.call-done = bf16[2048,1024]{1,0:T(8,128)(2,1)} async-done(((bf16[128,1024]{1,0:T(8,128)(2,1)}), bf16[2048,1024]{1,0:T(8,128)(2,1)}) %all-gather.15.cloned.1.call-update) | async-done | bytes 4194320 | tf_op jit(solution)/shard_map/all_gather | solution.py:42
  196.0 3.2 fusion.113
  199.2 2.8 multiply_convert_fusion.1
  202.1 2.4 multiply_convert_fusion.2
  204.5 1.4 all-gather.13.cloned.1.call-done
  205.8 4.4 fusion.52
  210.2 76.1 %all-gather.19.cloned.1.call-done = bf16[2048,1024]{1,0:T(8,128)(2,1)} async-done(((bf16[128,1024]{1,0:T(8,128)(2,1)}), bf16[2048,1024]{1,0:T(8,128)(2,1)}) %all-gather.19.cloned.1.call-update) | async-done | bytes 4194320 | tf_op jit(solution)/shard_map/all_gather | solution.py:42
  286.3 8.0 fusion.4
  294.4 2.9 multiply_convert_fusion
  297.4 6.0 fusion.2
  303.4 74.4 %all-reduce.6 = f32[16,3,128]{2,1,0:T(4,128)S(1)} all-reduce(f32[16,3,128]{2,1,0:T(4,128)S(1)} %pad_maximum_fusion.3), channel_id=8, replica_groups=mesh['dp'=2,'shard'=16] {'shard'}, use_global_device_ids=true, to_apply=%region_18.19.clone | all-reduce | flops 6144 | bytes 49152
  380.5 35.8 %all-gather.2 = f32[2048,3]{0,1:T(4,128)S(1)} all-gather(f32[128,3]{0,1:T(4,128)S(1)} %pad_maximum_fusion.4), channel_id=4, replica_groups=mesh['dp'=2,'shard'=16] {'shard'}, dimensions={0}, use_global_device_ids=true | all-gather | bytes 26112 | tf_op jit(solution)/shard_map/all_gather | solution.py:42
  416.4 10.2 %fusion.3 = (bf16[16,80,1024]{2,1,0:T(8,128)(2,1)S(1)}, bf16[16,80,1024]{2,1,0:T(8,128)(2,1)S(1)}, f32[16,80,1024]{2,1,0:T(8,128)}, f32[16,80,1024]{2,1,0:T(8,128)}) fusion(f32[16,80]{1,0:T(8,128)S(1)} %get-tuple-element.62, bf16[16,128,1024]{2,1,0:T(8,128)(2,1)} %bitcast.390, f32[16,80]{1,0:T(8,128)S(1)} %get-tuple-element.63, f32[16,80,1024]{2,1,0:T(8,128)} %fusion.52, ...), kind=kLoop, calls=%fused_computation.12 | loop fusion | flops 10485760 | bytes 31467520 | tf_op jit(solution)/shard_map/convert_element_type | solution.py:163
  426.6 1.4 fusion.8
  428.0 3.2 fusion.119
  431.2 1.4 fusion.9
  432.7 3.5 fusion.120
  436.2 1.9 copy-done.3
  438.2 7.0 fusion.1
  445.2 5.2 fusion.7
  451.4 2.9 add_convert_fusion
  454.9 92.5 %reduce-scatter.15.cloned.1.call-done = bf16[1,128,1024]{2,1,0:T(8,128)(2,1)} async-done(((bf16[16,128,1024]{2,1,0:T(8,128)(2,1)}), bf16[1,128,1024]{2,1,0:T(8,128)(2,1)}) %reduce-scatter.15.cloned.1.call-update) | async-done | bytes 262160 | tf_op jit(solution)/shard_map/reduce_scatter | solution.py:46
  547.4 1.7 multiply_reduce_fusion.1
  549.4 2.5 fusion.39
  552.1 1.7 multiply_reduce_fusion
  555.5 1.5 convolution_convert_fusion.1
  560.0 3.8 maximum_bitcast_fusion
  563.9 3.0 convolution_bitcast_fusion
  567.8 1.3 copy-done.7
  569.2 1.3 convolution_bitcast_fusion.2
  570.4 2.0 pad_maximum_fusion
  574.0 4.6 copy.102
  578.7 4.4 copy.103
  583.1 6.6 copy.101
  589.7 3.3 convolution_bitcast_fusion.4
  594.1 2.0 copy-done.8
  596.0 1.3 convolution_bitcast_fusion.5
  597.3 2.0 maximum_bitcast_fusion.1
  599.3 12.2 %all-reduce.17 = bf16[2,16,3,32,256]{4,3,1,0,2:T(8,128)(2,1)S(1)} all-reduce(f32[2,16,3,32,256]{4,3,1,0,2:T(8,128)} %maximum_bitcast_fusion.1), channel_id=11, replica_groups=mesh['dp'=2,'shard'=16] {'dp'}, use_global_device_ids=true, to_apply=%region_35.36.clone | all-reduce | flops 786432 | bytes 4718592
  613.2 5.7 all-to-all-start.1
  619.0 5.6 dynamic-slice_bitcast_fusion
  626.0 48.3 %psum.15 = s32[2]{0:T(128)S(1)} all-reduce(s32[2]{0:T(128)S(1)} %pad_add_fusion), channel_id=1, replica_groups=mesh['dp'=2,'shard'=16] {'dp','shard'}, use_global_device_ids=true, to_apply=%region_37.38 | all-reduce | flops 2 | bytes 16 | tf_op jit(solution)/shard_map/psum | solution.py:219
  674.8 2.0 reshape.306
  678.4 1.2 slice.251
  680.8 2.3 slice.285
  683.1 1.9 slice_bitcast_fusion.28
  685.0 2.4 fusion.17
  687.5 2.5 fusion.15
  690.0 2.6 multiply_reduce_fusion.6
  692.7 43.1 %psum.14 = f32[8,1024]{1,0:T(8,128)S(1)} all-reduce(f32[8,1024]{1,0:T(8,128)S(1)} %stack.176), channel_id=1, replica_groups=mesh['dp'=2,'shard'=16] {'dp','shard'}, use_global_device_ids=true, to_apply=%region_32.33 | all-reduce | flops 8192 | bytes 65536 | tf_op jit(solution)/shard_map/psum | solution.py:209
  737.6 2.0 convolution_convert_fusion.5
  740.6 156.4 %all-reduce.16.cloned.1.call-done = bf16[16,4,32,1024]{3,2,0,1:T(8,128)(2,1)} async-done(((bf16[16,4,32,1024]{3,2,0,1:T(8,128)(2,1)}), bf16[16,4,32,1024]{3,2,0,1:T(8,128)(2,1)}) %all-reduce.16.cloned.1.call-update) | async-done | bytes 4194320
  897.0 1.6 dynamic-slice_convert_fusion.1
  (239 shorter events, 34.9 us)
Async XLA Ops:
  7.2 98.4 %copy-start = (bf16[128,1024]{1,0:T(8,128)(2,1)S(1)}, bf16[128,1024]{1,0:T(8,128)(2,1)}, u32[]{:S(2)}) copy-start(bf16[128,1024]{1,0:T(8,128)(2,1)} %param.20) | copy-start | bytes 786436
  7.2 3.5 copy-start.38
  7.2 100.0 %all-gather.11.cloned.1.call-start = ((), (), s32[]{:S(2)}) async-start(), calls=%async_computation.5 | async-start | bytes 8650752 | tf_op jit(solution)/shard_map/all_gather | solution.py:109
  11.0 10.9 %copy-start.44 = (bf16[32,2]{0,1:T(2,128)(2,1)S(1)}, bf16[32,2]{0,1:T(2,128)(2,1)}, u32[]{:S(2)}) copy-start(bf16[32,2]{0,1:T(2,128)(2,1)} %param.36) | copy-start | bytes 388
  11.1 10.9 %copy-start.45 = (bf16[32,2]{0,1:T(2,128)(2,1)S(1)}, bf16[32,2]{0,1:T(2,128)(2,1)}, u32[]{:S(2)}) copy-start(bf16[32,2]{0,1:T(2,128)(2,1)} %param.35) | copy-start | bytes 388
  11.1 10.9 %copy-start.46 = (bf16[32]{0:T(256)(128)(2,1)S(1)}, bf16[32]{0:T(256)(128)(2,1)}, u32[]{:S(2)}) copy-start(bf16[32]{0:T(256)(128)(2,1)} %param.25) | copy-start | bytes 196
  11.1 10.9 %copy-start.47 = (bf16[32]{0:T(256)(128)(2,1)S(1)}, bf16[32]{0:T(256)(128)(2,1)}, u32[]{:S(2)}) copy-start(bf16[32]{0:T(256)(128)(2,1)} %param.26) | copy-start | bytes 196
  11.1 10.9 %copy-start.48 = (bf16[32]{0:T(256)(128)(2,1)S(1)}, bf16[32]{0:T(256)(128)(2,1)}, u32[]{:S(2)}) copy-start(bf16[32]{0:T(256)(128)(2,1)} %param.31) | copy-start | bytes 196
  11.1 10.9 %copy-start.49 = (bf16[32]{0:T(256)(128)(2,1)S(1)}, bf16[32]{0:T(256)(128)(2,1)}, u32[]{:S(2)}) copy-start(bf16[32]{0:T(256)(128)(2,1)} %param.32) | copy-start | bytes 196
  12.1 91.7 %copy-start.51 = (s32[128]{0:T(128)S(1)}, s32[128]{0:T(128)}, u32[]{:S(2)}) copy-start(s32[128]{0:T(128)} %param.22) | copy-start | bytes 1540
  12.2 92.3 %copy-start.50 = (s32[128]{0:T(128)S(1)}, s32[128]{0:T(128)}, u32[]{:S(2)}) copy-start(s32[128]{0:T(128)} %param.23) | copy-start | bytes 1540
  12.2 93.0 %copy-start.52 = (s32[1,128]{1,0:T(1,128)S(1)}, s32[1,128]{1,0:T(1,128)}, u32[]{:S(2)}) copy-start(s32[1,128]{1,0:T(1,128)} %param.21) | copy-start | bytes 1540
  13.6 92.6 %all-to-all-start = ((bf16[16,3,32,256]{3,2,1,0:T(8,128)(2,1)}), bf16[16,3,32,256]{3,2,1,0:T(8,128)(2,1)S(1)}, u32[]{:S(2)}, u32[]{:S(2)}) async-start(bf16[16,3,32,256]{3,2,1,0:T(8,128)(2,1)} %reshape.288), calls=%async_computation | async-start | bytes 1572864 | tf_op jit(solution)/shard_map/all_to_all | solution.py:113
  21.9 101.5 %all-gather.17.cloned.1.call-start = ((), (), s32[]{:S(2)}) async-start(), calls=%async_computation.11 | async-start | bytes 2359296 | tf_op jit(solution)/shard_map/all_gather | solution.py:114
  107.1 88.9 %all-gather.15.cloned.1.call-start = ((), (), s32[]{:S(2)}) async-start(), calls=%async_computation.10 | async-start | bytes 4456448 | tf_op jit(solution)/shard_map/all_gather | solution.py:42
  109.5 6.4 copy-start.26
  111.8 4.0 copy-start.28
  114.4 2.1 copy-start.39
  118.9 2.3 copy-start.37
  119.3 3.4 copy-start.55
  120.1 85.7 %all-gather.13.cloned.1.call-start = ((), (), s32[]{:S(2)}) async-start(), calls=%async_computation.6 | async-start | bytes 2359296 | tf_op jit(solution)/shard_map/all_gather | solution.py:117
  121.2 165.1 %all-gather.19.cloned.1.call-start = ((), (), s32[]{:S(2)}) async-start(), calls=%async_computation.12 | async-start | bytes 4456448 | tf_op jit(solution)/shard_map/all_gather | solution.py:42
  122.2 425.2 %reduce-scatter.15.cloned.1.call-start = ((), (), s32[]{:S(2)}) async-start(), calls=%async_computation.8 | async-start | bytes 4456448 | tf_op jit(solution)/shard_map/reduce_scatter | solution.py:46
  199.2 2.8 copy-start.5
  199.2 2.9 copy-start.6
  199.2 2.9 copy-start.17
  286.3 8.1 copy-start.4
  294.4 2.9 copy-start.2
  297.4 6.0 copy-start.21
  416.4 10.2 %copy-start.20 = (bf16[3,256,1024]{2,1,0:T(8,128)(2,1)S(1)}, bf16[3,256,1024]{2,1,0:T(8,128)(2,1)}, u32[]{:S(2)}) copy-start(bf16[3,256,1024]{2,1,0:T(8,128)(2,1)} %all-gather.13.cloned.1.call-done) | copy-start | bytes 4718596
  416.4 10.2 %copy-start.58 = (f32[1280,256]{1,0:T(8,128)S(1)}, f32[1280,256]{1,0:T(8,128)}, u32[]{:S(2)}) copy-start(f32[1280,256]{1,0:T(8,128)} %get-tuple-element.97) | copy-start | bytes 3932164
  426.5 4.7 copy-start.12
  428.0 3.2 copy-start.33
  428.0 3.2 copy-start.57
  431.2 5.0 slice-start
  431.2 5.0 slice-start.1
  432.7 3.6 copy-start.34
  432.7 5.5 copy-start.3
  445.1 6.2 slice-start.2
  445.1 6.2 slice-start.4
  445.1 6.2 slice-start.3
  445.1 6.2 slice-start.5
  454.3 94.8 %copy-start.14 = (bf16[128,1024]{1,0:T(8,128)(2,1)S(1)}, bf16[128,1024]{1,0:T(8,128)(2,1)}, u32[]{:S(2)}) copy-start(bf16[128,1024]{1,0:T(8,128)(2,1)} %convolution_convert_fusion.4) | copy-start | bytes 786436
  454.3 164.6 %all-reduce.14.cloned.1.call-start = ((), (), s32[]{:S(2)}) async-start(), calls=%async_computation.13 | async-start | bytes 16777216
  549.4 2.7 copy-start.40
  555.5 2.2 copy-start.30
  563.9 116.9 %reduce-scatter.17.cloned.1.call-start = ((), (), s32[]{:S(2)}) async-start(), calls=%async_computation.9 | async-start | bytes 4718592 | tf_op jit(solution)/shard_map/reduce_scatter | solution.py:214
  563.9 3.0 copy-start.11
  563.9 3.0 copy-start.32
  563.9 3.9 copy-start.22
  566.9 2.2 copy-start.7
  572.5 165.1 %reduce-scatter.13.cloned.1.call-start = ((), (), s32[]{:S(2)}) async-start(), calls=%async_computation.7 | async-start | bytes 4456448 | tf_op jit(solution)/shard_map/reduce_scatter | solution.py:46
  589.7 3.3 copy-start.13
  589.7 3.5 copy-start.35
  589.7 4.4 copy-start.24
  593.2 2.8 copy-start.8
  613.2 61.6 %all-to-all-start.1 = ((bf16[16,3,32,256]{3,2,1,0:T(8,128)(2,1)}), bf16[16,3,32,256]{3,2,1,0:T(8,128)(2,1)}, u32[]{:S(2)}, u32[]{:S(2)}) async-start(bf16[16,3,32,256]{3,2,1,0:T(8,128)(2,1)} %copy.104), calls=%async_computation.3 | async-start | bytes 1572864 | tf_op jit(solution)/shard_map/all_to_all | solution.py:217
  618.9 278.1 %all-reduce.16.cloned.1.call-start = ((), (), s32[]{:S(2)}) async-start(), calls=%async_computation.14 | async-start | bytes 8388608
  624.6 49.7 %copy-start.53 = (f32[2]{0:T(128)S(1)}, f32[2]{0:T(128)}, u32[]{:S(2)}) copy-start(f32[2]{0:T(128)} %param.39) | copy-start | bytes 28
  674.3 2.7 copy-start.56
  679.9 5.2 copy-start.31
  683.1 4.4 copy-start.43
  687.5 2.5 copy-start.16
  737.6 161.9 %copy-start.1 = (bf16[128,1024]{1,0:T(8,128)(2,1)S(1)}, bf16[128,1024]{1,0:T(8,128)(2,1)}, u32[]{:S(2)}) copy-start(bf16[128,1024]{1,0:T(8,128)(2,1)} %param.20) | copy-start | bytes 786436
  (13 other events, 16.9 us)
Sparse Core Ops, SparseCore 0:
  11.5 86.9 all-gather.10
  107.2 8.1 all-gather.16
  120.2 75.7 all-gather.14
  197.4 8.3 all-gather.12
  209.0 77.2 all-gather.18
  454.4 92.9 reduce-scatter.14
  564.0 38.4 all-reduce.13
  604.7 12.2 reduce-scatter.16
  619.4 101.9 reduce-scatter.12
  727.8 169.1 all-reduce.15
where the time goes:
time: 914 us; the launch traced here: 907 us
  waiting for transfers between devices  397 us (43%)
  blocking collectives  296 us (32%)
  matrix products  86.9 us (10%)
  local copies, waits for them, and re-layouts  55.6 us (6%)
  other arithmetic  40 us (4%)
  between operations  16.4 us (2%)
  starting transfers between devices  15.4 us (2%)
    unnamed x12, waiting for transfers between devices  157 us
    all_gather x2, waiting for transfers between devices, ag(): return lax.all_gather(block, 'shard', axis=0, tiled=False)  146 us
    reduce_scatter x2, waiting for transfers between devices, rs(): lax.psum_scatter(parts.astype(BF), 'shard', scatter_dimension=0, tiled=Fa...  92.5 us
    unnamed x2, blocking collectives  86.7 us
    all_gather x1, blocking collectives, body(): small = lax.all_gather(small, BOTH, axis=1, tiled=True)  81.6 us
    dot_general x35, matrix products, mm(): return lax.dot_general(a, b, (dims, ((), ())), preferred_element_type=F32)  80.9 us
    psum x1, blocking collectives, body(): counts = lax.psum(jnp.stack([n0, T - n0]), BOTH)  48.3 us
    psum x1, blocking collectives, body(): smalls = lax.psum(jnp.stack([gg1, gb1, gg2, gb2] + gw), BOTH)  43.1 us
  transfers between devices with their start and end apart: 12, of which 5 were waited for; matrix products, arithmetic and copies ran while one was open for 11% of the time, Pallas kernels for 0%

commit v1 on v0

--- a/solution.py
+++ b/solution.py
@@ -216,7 +216,7 @@
     gup = lax.psum_scatter(gup, "dp", scatter_dimension=0, tiled=False).astype(BF)
     gup = lax.all_to_all(gup, "shard", 0, 0).astype(F32)
     gup = gup.reshape(S, 3, WR, C, FR).transpose(1, 2, 3, 0, 4).reshape(3, WR, FF)
-    counts = lax.psum(jnp.stack([n0, T - n0]), BOTH)
+    counts = lax.psum(lax.psum(jnp.stack([n0, T - n0]), "shard"), "dp")
     load_new = 0.9 * load_avg + 0.1 * counts.astype(F32) * E / (T * C * S)
     return (
         layer_out,

time: 914 us -> 913 us (level)
  blocking collectives: 296 us -> 269 us
  waiting for transfers between devices: 397 us -> 423 us
    psum x1 -> x2, blocking collectives: 48.3 us -> 20.6 us  [body(): counts = lax.psum(lax.psum(jnp.stack([n0, T - n0]), 'shard'), 'dp')]
    unnamed x12, waiting for transfers between devices: 157 us -> 173 us
    reduce_scatter x2, waiting for transfers between devices: 92.5 us -> 102 us  [rs(): lax.psum_scatter(parts.astype(BF), 'shard', scatter_dimension=0, tiled=Fa...]
  transfers between devices with their start and end apart: 12 -> 12, of which waited for: 5 -> 6; matrix products, arithmetic and copies ran while one was open for 11% -> 11% of each run, Pallas kernels for 0% -> 0%
where the time goes in v1:
time: 913 us; the launch traced here: 906 us
  waiting for transfers between devices  423 us (46%)
  blocking collectives  269 us (29%)
  matrix products  86.9 us (10%)
  local copies, waits for them, and re-layouts  55.4 us (6%)
  other arithmetic  40 us (4%)
  between operations  16.4 us (2%)
  starting transfers between devices  15.5 us (2%)
    unnamed x12, waiting for transfers between devices  173 us
    all_gather x2, waiting for transfers between devices, ag(): return lax.all_gather(block, 'shard', axis=0, tiled=False)  146 us
    reduce_scatter x2, waiting for transfers between devices, rs(): lax.psum_scatter(parts.astype(BF), 'shard', scatter_dimension=0, tiled=Fa...  102 us
    unnamed x2, blocking collectives  86.7 us
    all_gather x1, blocking collectives, body(): small = lax.all_gather(small, BOTH, axis=1, tiled=True)  81.6 us
    dot_general x35, matrix products, mm(): return lax.dot_general(a, b, (dims, ((), ())), preferred_element_type=F32)  80.9 us
    psum x1, blocking collectives, body(): smalls = lax.psum(jnp.stack([gg1, gb1, gg2, gb2] + gw), BOTH)  44.2 us
    all_gather x1, blocking collectives, ag(): return lax.all_gather(block, 'shard', axis=0, tiled=False)  35.8 us
  transfers between devices with their start and end apart: 12, of which 6 were waited for; matrix products, arithmetic and copies ran while one was open for 11% of the time, Pallas kernels for 0%

profile of v1, /device:TPU:0, one launch (start us, length us, event | category | flops | bytes accessed | tf_op | source)
XLA Modules:
  0.0 906.3 jit_solution(8733417576058844713)
XLA Ops:
  7.3 1.7 pad_maximum_fusion.2
  12.2 1.4 reshape.288
  13.6 8.3 all-to-all-start
  22.1 81.6 %all-gather.4 = f32[32,32,8]{1,2,0:T(8,128)S(1)} all-gather(f32[1,32,8]{1,2,0:T(8,128)S(1)} %convert_bitcast_fusion.4), channel_id=1, replica_groups=mesh['dp'=2,'shard'=16] {'dp','shard'}, dimensions={0}, use_global_device_ids=true | all-gather | bytes 33792 | tf_op jit(solution)/shard_map/all_gather | solution.py:105
  107.2 2.1 fusion.40
  109.5 2.2 fusion.42
  111.8 2.4 fusion.41
  114.4 1.5 fusion.117
  116.6 2.1 fusion.118
  123.3 1.6 copy.132
  125.9 70.1 %all-gather.15.cloned.1.call-done = bf16[2048,1024]{1,0:T(8,128)(2,1)} async-done(((bf16[128,1024]{1,0:T(8,128)(2,1)}), bf16[2048,1024]{1,0:T(8,128)(2,1)}) %all-gather.15.cloned.1.call-update) | async-done | bytes 4194320 | tf_op jit(solution)/shard_map/all_gather | solution.py:42
  196.0 3.2 fusion.113
  199.2 2.8 multiply_convert_fusion.1
  202.1 2.3 multiply_convert_fusion.2
  204.4 1.4 all-gather.13.cloned.1.call-done
  205.8 4.4 fusion.52
  210.2 76.1 %all-gather.19.cloned.1.call-done = bf16[2048,1024]{1,0:T(8,128)(2,1)} async-done(((bf16[128,1024]{1,0:T(8,128)(2,1)}), bf16[2048,1024]{1,0:T(8,128)(2,1)}) %all-gather.19.cloned.1.call-update) | async-done | bytes 4194320 | tf_op jit(solution)/shard_map/all_gather | solution.py:42
  286.3 8.0 fusion.4
  294.4 2.9 multiply_convert_fusion
  297.4 6.0 fusion.2
  303.4 74.4 %all-reduce.6 = f32[16,3,128]{2,1,0:T(4,128)S(1)} all-reduce(f32[16,3,128]{2,1,0:T(4,128)S(1)} %pad_maximum_fusion.3), channel_id=8, replica_groups=mesh['dp'=2,'shard'=16] {'shard'}, use_global_device_ids=true, to_apply=%region_18.19.clone | all-reduce | flops 6144 | bytes 49152
  380.5 35.8 %all-gather.2 = f32[2048,3]{0,1:T(4,128)S(1)} all-gather(f32[128,3]{0,1:T(4,128)S(1)} %pad_maximum_fusion.4), channel_id=4, replica_groups=mesh['dp'=2,'shard'=16] {'shard'}, dimensions={0}, use_global_device_ids=true | all-gather | bytes 26112 | tf_op jit(solution)/shard_map/all_gather | solution.py:42
  416.4 10.2 %fusion.3 = (bf16[16,80,1024]{2,1,0:T(8,128)(2,1)S(1)}, bf16[16,80,1024]{2,1,0:T(8,128)(2,1)S(1)}, f32[16,80,1024]{2,1,0:T(8,128)}, f32[16,80,1024]{2,1,0:T(8,128)}) fusion(f32[16,80]{1,0:T(8,128)S(1)} %get-tuple-element.62, bf16[16,128,1024]{2,1,0:T(8,128)(2,1)} %bitcast.390, f32[16,80]{1,0:T(8,128)S(1)} %get-tuple-element.63, f32[16,80,1024]{2,1,0:T(8,128)} %fusion.52, ...), kind=kLoop, calls=%fused_computation.12 | loop fusion | flops 10485760 | bytes 31467520 | tf_op jit(solution)/shard_map/convert_element_type | solution.py:163
  426.6 1.4 fusion.8
  428.1 3.2 fusion.119
  431.3 1.4 fusion.9
  432.7 3.5 fusion.120
  436.3 1.9 copy-done.3
  438.2 7.0 fusion.1
  445.2 5.2 fusion.7
  451.4 2.9 add_convert_fusion
  455.0 92.5 %reduce-scatter.15.cloned.1.call-done = bf16[1,128,1024]{2,1,0:T(8,128)(2,1)} async-done(((bf16[16,128,1024]{2,1,0:T(8,128)(2,1)}), bf16[1,128,1024]{2,1,0:T(8,128)(2,1)}) %reduce-scatter.15.cloned.1.call-update) | async-done | bytes 262160 | tf_op jit(solution)/shard_map/reduce_scatter | solution.py:46
  547.4 1.7 multiply_reduce_fusion.1
  549.4 2.5 fusion.39
  552.1 1.7 multiply_reduce_fusion
  555.5 1.5 convolution_convert_fusion.1
  560.1 3.8 maximum_bitcast_fusion
  564.0 3.0 convolution_bitcast_fusion
  567.9 1.3 copy-done.7
  569.2 1.3 convolution_bitcast_fusion.2
  570.5 2.1 pad_maximum_fusion
  574.1 4.6 copy.102
  578.7 4.4 copy.103
  583.1 6.5 copy.101
  589.7 3.3 convolution_bitcast_fusion.4
  594.0 1.9 copy-done.8
  596.0 1.3 convolution_bitcast_fusion.5
  597.2 2.0 maximum_bitcast_fusion.1
  599.2 12.2 %all-reduce.17 = bf16[2,16,3,32,256]{4,3,1,0,2:T(8,128)(2,1)S(1)} all-reduce(f32[2,16,3,32,256]{4,3,1,0,2:T(8,128)} %maximum_bitcast_fusion.1), channel_id=11, replica_groups=mesh['dp'=2,'shard'=16] {'dp'}, use_global_device_ids=true, to_apply=%region_35.36.clone | all-reduce | flops 786432 | bytes 4718592
  613.1 5.8 all-to-all-start.1
  619.0 5.6 dynamic-slice_bitcast_fusion
  626.0 18.8 %psum.22 = s32[2]{0:T(128)S(1)} all-reduce(s32[2]{0:T(128)S(1)} %pad_add_fusion), channel_id=1, replica_groups=mesh['dp'=2,'shard'=16] {'shard'}, use_global_device_ids=true, to_apply=%region_37.38 | all-reduce | flops 2 | bytes 16 | tf_op jit(solution)/shard_map/psum | solution.py:219
  644.8 1.8 psum.23
  647.2 2.0 reshape.306
  653.1 2.3 slice.285
  655.5 1.9 slice_bitcast_fusion.28
  657.4 2.4 fusion.17
  659.8 2.5 fusion.15
  662.3 2.6 multiply_reduce_fusion.6
  665.0 44.2 %psum.21 = f32[8,1024]{1,0:T(8,128)S(1)} all-reduce(f32[8,1024]{1,0:T(8,128)S(1)} %stack.176), channel_id=1, replica_groups=mesh['dp'=2,'shard'=16] {'dp','shard'}, use_global_device_ids=true, to_apply=%region_32.33 | all-reduce | flops 8192 | bytes 65536 | tf_op jit(solution)/shard_map/psum | solution.py:209
  711.0 9.9 %reduce-scatter.13.cloned.1.call-done = bf16[1,128,1024]{2,1,0:T(8,128)(2,1)} async-done(((bf16[16,128,1024]{2,1,0:T(8,128)(2,1)}), bf16[1,128,1024]{2,1,0:T(8,128)(2,1)}) %reduce-scatter.13.cloned.1.call-update) | async-done | bytes 262160 | tf_op jit(solution)/shard_map/reduce_scatter | solution.py:46
  720.8 2.0 convolution_convert_fusion.5
  723.9 172.6 %all-reduce.16.cloned.1.call-done = bf16[16,4,32,1024]{3,2,0,1:T(8,128)(2,1)} async-done(((bf16[16,4,32,1024]{3,2,0,1:T(8,128)(2,1)}), bf16[16,4,32,1024]{3,2,0,1:T(8,128)(2,1)}) %all-reduce.16.cloned.1.call-update) | async-done | bytes 4194320
  896.6 1.6 dynamic-slice_convert_fusion.1
  (240 shorter events, 37.2 us)
Async XLA Ops:
  7.2 98.4 %copy-start = (bf16[128,1024]{1,0:T(8,128)(2,1)S(1)}, bf16[128,1024]{1,0:T(8,128)(2,1)}, u32[]{:S(2)}) copy-start(bf16[128,1024]{1,0:T(8,128)(2,1)} %param.20) | copy-start | bytes 786436
  7.2 3.5 copy-start.38
  7.2 100.0 %all-gather.11.cloned.1.call-start = ((), (), s32[]{:S(2)}) async-start(), calls=%async_computation.5 | async-start | bytes 8650752 | tf_op jit(solution)/shard_map/all_gather | solution.py:109
  11.0 10.9 %copy-start.44 = (bf16[32,2]{0,1:T(2,128)(2,1)S(1)}, bf16[32,2]{0,1:T(2,128)(2,1)}, u32[]{:S(2)}) copy-start(bf16[32,2]{0,1:T(2,128)(2,1)} %param.36) | copy-start | bytes 388
  11.1 10.9 %copy-start.45 = (bf16[32,2]{0,1:T(2,128)(2,1)S(1)}, bf16[32,2]{0,1:T(2,128)(2,1)}, u32[]{:S(2)}) copy-start(bf16[32,2]{0,1:T(2,128)(2,1)} %param.35) | copy-start | bytes 388
  11.1 10.9 %copy-start.46 = (bf16[32]{0:T(256)(128)(2,1)S(1)}, bf16[32]{0:T(256)(128)(2,1)}, u32[]{:S(2)}) copy-start(bf16[32]{0:T(256)(128)(2,1)} %param.25) | copy-start | bytes 196
  11.1 10.9 %copy-start.47 = (bf16[32]{0:T(256)(128)(2,1)S(1)}, bf16[32]{0:T(256)(128)(2,1)}, u32[]{:S(2)}) copy-start(bf16[32]{0:T(256)(128)(2,1)} %param.26) | copy-start | bytes 196
  11.1 10.9 %copy-start.48 = (bf16[32]{0:T(256)(128)(2,1)S(1)}, bf16[32]{0:T(256)(128)(2,1)}, u32[]{:S(2)}) copy-start(bf16[32]{0:T(256)(128)(2,1)} %param.31) | copy-start | bytes 196
  11.1 10.9 %copy-start.49 = (bf16[32]{0:T(256)(128)(2,1)S(1)}, bf16[32]{0:T(256)(128)(2,1)}, u32[]{:S(2)}) copy-start(bf16[32]{0:T(256)(128)(2,1)} %param.32) | copy-start | bytes 196
  12.1 91.7 %copy-start.51 = (s32[128]{0:T(128)S(1)}, s32[128]{0:T(128)}, u32[]{:S(2)}) copy-start(s32[128]{0:T(128)} %param.22) | copy-start | bytes 1540
  12.2 92.3 %copy-start.50 = (s32[128]{0:T(128)S(1)}, s32[128]{0:T(128)}, u32[]{:S(2)}) copy-start(s32[128]{0:T(128)} %param.23) | copy-start | bytes 1540
  12.2 93.0 %copy-start.52 = (s32[1,128]{1,0:T(1,128)S(1)}, s32[1,128]{1,0:T(1,128)}, u32[]{:S(2)}) copy-start(s32[1,128]{1,0:T(1,128)} %param.21) | copy-start | bytes 1540
  13.6 92.6 %all-to-all-start = ((bf16[16,3,32,256]{3,2,1,0:T(8,128)(2,1)}), bf16[16,3,32,256]{3,2,1,0:T(8,128)(2,1)S(1)}, u32[]{:S(2)}, u32[]{:S(2)}) async-start(bf16[16,3,32,256]{3,2,1,0:T(8,128)(2,1)} %reshape.288), calls=%async_computation | async-start | bytes 1572864 | tf_op jit(solution)/shard_map/all_to_all | solution.py:113
  21.9 101.5 %all-gather.17.cloned.1.call-start = ((), (), s32[]{:S(2)}) async-start(), calls=%async_computation.11 | async-start | bytes 2359296 | tf_op jit(solution)/shard_map/all_gather | solution.py:114
  107.1 88.9 %all-gather.15.cloned.1.call-start = ((), (), s32[]{:S(2)}) async-start(), calls=%async_computation.10 | async-start | bytes 4456448 | tf_op jit(solution)/shard_map/all_gather | solution.py:42
  109.5 6.4 copy-start.26
  111.8 4.0 copy-start.28
  114.4 2.1 copy-start.39
  118.9 2.3 copy-start.37
  119.3 3.4 copy-start.55
  120.1 85.7 %all-gather.13.cloned.1.call-start = ((), (), s32[]{:S(2)}) async-start(), calls=%async_computation.6 | async-start | bytes 2359296 | tf_op jit(solution)/shard_map/all_gather | solution.py:117
  121.2 165.1 %all-gather.19.cloned.1.call-start = ((), (), s32[]{:S(2)}) async-start(), calls=%async_computation.12 | async-start | bytes 4456448 | tf_op jit(solution)/shard_map/all_gather | solution.py:42
  122.2 425.2 %reduce-scatter.15.cloned.1.call-start = ((), (), s32[]{:S(2)}) async-start(), calls=%async_computation.8 | async-start | bytes 4456448 | tf_op jit(solution)/shard_map/reduce_scatter | solution.py:46
  199.2 2.8 copy-start.5
  199.2 2.9 copy-start.6
  199.2 2.9 copy-start.17
  286.3 8.1 copy-start.4
  294.4 2.9 copy-start.2
  297.4 6.0 copy-start.21
  416.4 10.2 %copy-start.20 = (bf16[3,256,1024]{2,1,0:T(8,128)(2,1)S(1)}, bf16[3,256,1024]{2,1,0:T(8,128)(2,1)}, u32[]{:S(2)}) copy-start(bf16[3,256,1024]{2,1,0:T(8,128)(2,1)} %all-gather.13.cloned.1.call-done) | copy-start | bytes 4718596
  416.4 10.2 %copy-start.58 = (f32[1280,256]{1,0:T(8,128)S(1)}, f32[1280,256]{1,0:T(8,128)}, u32[]{:S(2)}) copy-start(f32[1280,256]{1,0:T(8,128)} %get-tuple-element.97) | copy-start | bytes 3932164
  426.6 4.7 copy-start.12
  428.1 3.2 copy-start.33
  428.1 3.2 copy-start.57
  431.3 5.0 slice-start
  431.3 5.0 slice-start.1
  432.7 3.6 copy-start.34
  432.7 5.5 copy-start.3
  445.2 6.2 slice-start.2
  445.2 6.2 slice-start.4
  445.2 6.2 slice-start.3
  445.2 6.2 slice-start.5
  454.4 94.8 %copy-start.14 = (bf16[128,1024]{1,0:T(8,128)(2,1)S(1)}, bf16[128,1024]{1,0:T(8,128)(2,1)}, u32[]{:S(2)}) copy-start(bf16[128,1024]{1,0:T(8,128)(2,1)} %convolution_convert_fusion.4) | copy-start | bytes 786436
  454.4 164.6 %all-reduce.14.cloned.1.call-start = ((), (), s32[]{:S(2)}) async-start(), calls=%async_computation.13 | async-start | bytes 16777216
  549.4 2.7 copy-start.40
  555.5 2.2 copy-start.30
  563.9 89.2 %reduce-scatter.17.cloned.1.call-start = ((), (), s32[]{:S(2)}) async-start(), calls=%async_computation.9 | async-start | bytes 4718592 | tf_op jit(solution)/shard_map/reduce_scatter | solution.py:214
  563.9 3.0 copy-start.11
  564.0 3.0 copy-start.32
  564.0 3.9 copy-start.22
  567.0 2.2 copy-start.7
  572.6 148.3 %reduce-scatter.13.cloned.1.call-start = ((), (), s32[]{:S(2)}) async-start(), calls=%async_computation.7 | async-start | bytes 4456448 | tf_op jit(solution)/shard_map/reduce_scatter | solution.py:46
  589.7 3.3 copy-start.13
  589.7 3.5 copy-start.35
  589.7 4.4 copy-start.24
  593.2 2.8 copy-start.8
  613.1 34.0 %all-to-all-start.1 = ((bf16[16,3,32,256]{3,2,1,0:T(8,128)(2,1)}), bf16[16,3,32,256]{3,2,1,0:T(8,128)(2,1)}, u32[]{:S(2)}, u32[]{:S(2)}) async-start(bf16[16,3,32,256]{3,2,1,0:T(8,128)(2,1)} %copy.104), calls=%async_computation.3 | async-start | bytes 1572864 | tf_op jit(solution)/shard_map/all_to_all | solution.py:217
  618.9 277.6 %all-reduce.16.cloned.1.call-start = ((), (), s32[]{:S(2)}) async-start(), calls=%async_computation.14 | async-start | bytes 8388608
  624.6 22.0 %copy-start.53 = (f32[2]{0:T(128)S(1)}, f32[2]{0:T(128)}, u32[]{:S(2)}) copy-start(f32[2]{0:T(128)} %param.39) | copy-start | bytes 28
  646.6 2.7 copy-start.56
  652.2 5.2 copy-start.31
  655.5 4.4 copy-start.43
  659.8 2.5 copy-start.16
  720.8 178.2 %copy-start.1 = (bf16[128,1024]{1,0:T(8,128)(2,1)S(1)}, bf16[128,1024]{1,0:T(8,128)(2,1)}, u32[]{:S(2)}) copy-start(bf16[128,1024]{1,0:T(8,128)(2,1)} %param.20) | copy-start | bytes 786436
  (13 other events, 16.9 us)
Sparse Core Ops, SparseCore 0:
  11.5 86.9 all-gather.10
  107.2 8.1 all-gather.16
  120.2 75.7 all-gather.14
  197.4 8.3 all-gather.12
  209.0 77.2 all-gather.18
  454.5 92.9 reduce-scatter.14
  564.0 38.4 all-reduce.13
  604.7 12.2 reduce-scatter.16
  619.5 101.3 reduce-scatter.12
  727.3 169.2 all-reduce.15
